TPU v7x, 128 devices: a whole 4x4x4 slice. The times are simulated.
128 devices in a mesh: seq: 32 (over z, y, core), tp: 4 (over x).
Axes of the slice: x: 4, y: 4, z: 4, core: 2. Of those that a mesh axis runs over, the one named last changes fastest.
Arguments:
- tokens: bfloat16 [32768, 2048], P('seq', 'tp'), may hold values from -8 to 8
- col_order: int32 [32768], P('seq'), may hold values from 0 to 32767, as said below
- in_gain: float32 [2, 2048], replicated, may hold values from 0.5 to 1.5
- w_in: bfloat16 [2, 2048, 2, 2048], P(None, None, None, 'tp'), may hold values from -0.125 to 0.125
- w_bc: bfloat16 [2, 2048, 256], replicated, may hold values from -0.0625 to 0.0625
- w_dt: bfloat16 [2, 2048, 32], P(None, None, 'tp'), may hold values from -2 to 2
- conv_x: float32 [2, 4, 2048], P(None, None, 'tp'), may hold values from -3 to 3
- conv_bc: float32 [2, 4, 256], replicated, may hold values from -3 to 3
- dt_bias: float32 [2, 32], P(None, 'tp'), may hold values from -1 to 0.5
- a_log: float32 [2, 32], P(None, 'tp'), may hold values from -16 to -2, as said below
- d_skip: float32 [2, 32], P(None, 'tp'), may hold values from 0.5 to 2
- out_gain: float32 [2, 2048], P(None, 'tp'), may hold values from 0.5 to 1.5
- w_out: bfloat16 [2, 2048, 2048], P(None, 'tp'), may hold values from -0.125 to 0.125
Outputs:
- mixed_out: bfloat16 [32768, 2048], P('seq', 'tp')
Inputs may be any that keep to these rules, and one draw needn't show every extreme that they name: `col_order`: A permutation of the 32768 positions of a frame of 64 rows and 512 columns stored row by row: the column order visits the columns one after another in a drawn order, each from top to bottom or from bottom to top as drawn. So every aligned block of 1024 positions takes exactly 32 row-order positions from each aligned block of 1024 row-order positions. Each head's decay rate exp(a_log) is either between about one in fifty and one in seventeen a step or between 0.3 / 32768 and 2 / 32768 a step.
All inputs are finite; a program needn't handle non-finite values.
Results may differ from a plain program's by a relative error of at most 0.024.
Values may be sent and summed in bfloat16 or wider, within the bound.
No kernel may reach another device: no remote copies, remote signals or barrier semaphores. Data moves between devices by JAX's collectives and lax.ppermute only.
A program may use at most 128 MiB of HBM per device.

v0:
```python
import jax
import jax.numpy as jnp
from jax import lax
from jax.sharding import Mesh
from jax.sharding import PartitionSpec as P

HEAD_DIM = 64
STATE = 128
STRETCH = 128
SEQ = ("seq_0", "seq_1", "seq_2")
highest = lax.Precision.HIGHEST
epsilon = 1e-05


def laid_out(blocks, dim):
    blocks = jnp.moveaxis(blocks, 0, dim)
    lengths = blocks.shape
    return blocks.reshape(*lengths[:dim], lengths[dim] * lengths[dim + 1], *lengths[dim + 2 :])


def sent_to_all(x, axis):
    devices = lax.axis_size(axis)
    return lax.all_to_all(jnp.broadcast_to(x[None], (devices, *x.shape)), axis, 0, 0, tiled=True)


def gathered_copies(x, axis, dim):
    return laid_out(sent_to_all(x, axis), dim)


def passed_along(x, axis, by):
    devices = lax.axis_size(axis)
    pairs = [(i, i + by) for i in range(devices) if 0 <= i + by < devices]
    return lax.ppermute(x, axis, pairs)


def in_blocks(x, dim, devices):
    lengths = x.shape
    blocks = x.reshape(*lengths[:dim], devices, lengths[dim] // devices, *lengths[dim + 1 :])
    return jnp.moveaxis(blocks, dim, 0)


def moved_by_axis(blocks, axes, turns):
    lengths = [lax.axis_size(a) for a in axes]
    blocks = blocks.reshape(*lengths, *blocks.shape[1:])
    for k in turns:
        blocks = lax.all_to_all(blocks, axes[k], split_axis=k, concat_axis=k, tiled=True)
    return blocks.reshape(-1, *blocks.shape[len(axes) :])


def exchange_by_chip(x, groups, turns, split_dim, concat_dim):
    devices = lax.axis_size(groups[0]) * lax.axis_size(groups[1])
    blocks = in_blocks(x, split_dim, devices)
    return laid_out(moved_by_axis(blocks, groups, turns), concat_dim)


def causal_mix(current, rim, taps):
    length = current.shape[0]
    extended = jnp.concatenate([rim, current], axis=0).astype(jnp.float32)
    mixed = jnp.zeros(current.shape, jnp.float32)
    for offset in range(taps.shape[0]):
        mixed = mixed + taps[offset] * extended[offset : offset + length]
    return mixed


def advance(state, pieces):
    factor, fresh = pieces
    return (factor[:, None, None] * state + fresh, state)


def incoming_state(local_end, device_log):
    count = lax.axis_size(SEQ)
    own_index = lax.axis_index(SEQ)
    gathered = gathered_copies(device_log, SEQ, 0).reshape(count, device_log.shape[0])
    before = jnp.cumsum(gathered, axis=0) - gathered
    earlier = (jnp.arange(count) < own_index)[:, None]
    own_prefix = jnp.sum(jnp.where(earlier, gathered, 0.0), axis=0)
    spans = jnp.where(earlier, own_prefix[None, :] - before - gathered, -jnp.inf)
    factors = jnp.exp(spans)
    return jnp.zeros(local_end.shape, jnp.float32) + jnp.einsum(
        "mh,mhpn->hpn",
        factors,
        lax.all_gather(local_end[None].astype(jnp.bfloat16), SEQ, axis=0, tiled=True).astype(
            jnp.float32
        ),
        precision=highest,
    )


def mixer(full, which, params):
    in_gain, w_in, w_bc, w_dt, conv_x, conv_bc, dt_bias, a_log, d_skip, out_gain, w_out = params
    row_count, model_width = full.shape
    inner = w_in.shape[3]
    head_count = inner // HEAD_DIM
    lag = conv_x.shape[1] - 1
    widen = full.astype(jnp.float32)
    scale = lax.rsqrt(jnp.mean(widen * widen, axis=-1, keepdims=True) + epsilon)
    normed = (widen * scale * in_gain[which]).astype(jnp.bfloat16)
    projected = jnp.dot(
        normed, w_in[which].reshape(model_width, 2 * inner), preferred_element_type=jnp.float32
    )
    pre_x = projected[:, :inner].astype(jnp.bfloat16)
    gate_z = projected[:, inner:].astype(jnp.bfloat16)
    pre_bc = jnp.dot(normed, w_bc[which], preferred_element_type=jnp.float32).astype(jnp.bfloat16)
    dt_raw = jnp.dot(normed, w_dt[which], preferred_element_type=jnp.float32)
    rim_x, rim_bc = passed_along((pre_x[row_count - lag :], pre_bc[row_count - lag :]), SEQ, 1)
    conv_out = jax.nn.silu(causal_mix(pre_x, rim_x, conv_x[which]))
    bc_out = jax.nn.silu(causal_mix(pre_bc, rim_bc, conv_bc[which]))
    step_size = jax.nn.softplus(dt_raw + dt_bias[which])
    decay_log = -step_size * jnp.exp(a_log[which])
    heads_in = conv_out.reshape(row_count, head_count, HEAD_DIM)
    feed = heads_in * step_size[:, :, None]
    blocks = row_count // STRETCH
    log_blocks = decay_log.reshape(blocks, STRETCH, head_count)
    b_blocks = bc_out[:, :STATE].reshape(blocks, STRETCH, STATE)
    c_blocks = bc_out[:, STATE:].reshape(blocks, STRETCH, STATE)
    feed_blocks = feed.reshape(blocks, STRETCH, head_count, HEAD_DIM)
    cumul = jnp.cumsum(log_blocks, axis=1)
    cumul_t = jnp.transpose(cumul, (0, 2, 1))
    lower = jnp.arange(STRETCH)[:, None] >= jnp.arange(STRETCH)[None, :]
    spread = jnp.where(lower[None, None], cumul_t[..., :, None] - cumul_t[..., None, :], -jnp.inf)
    intersection = jnp.einsum("cqn,ckn->cqk", c_blocks, b_blocks, precision=highest)
    inside = jnp.einsum(
        "chqk,ckhp->cqhp", intersection[:, None] * jnp.exp(spread), feed_blocks, precision=highest
    )
    to_end = jnp.exp(cumul_t[..., -1:] - cumul_t)
    fresh = jnp.einsum("chk,ckn,ckhp->chpn", to_end, b_blocks, feed_blocks, precision=highest)
    block_decay = jnp.exp(cumul_t[..., -1])
    start_state = jnp.zeros((head_count, HEAD_DIM, STATE), jnp.float32)
    local_end, entering = lax.scan(advance, start_state, (block_decay, fresh))
    carried = (
        jnp.einsum("cqn,chpn->cqhp", c_blocks, entering, precision=highest)
        * jnp.exp(cumul)[..., None]
    )
    block_sums = cumul[:, -1, :]
    prior = jnp.cumsum(block_sums, axis=0) - block_sums
    device_cumul = cumul + prior[:, None, :]
    device_log = jnp.sum(block_sums, axis=0)
    arriving = incoming_state(local_end, device_log)
    correction = (
        jnp.einsum("cqn,hpn->cqhp", c_blocks, arriving, precision=highest)
        * jnp.exp(device_cumul)[..., None]
    )
    ssd = (inside + carried + correction).reshape(row_count, head_count, HEAD_DIM) + d_skip[which][
        None, :, None
    ] * heads_in
    gated = ssd * jax.nn.silu(gate_z.astype(jnp.float32).reshape(row_count, head_count, HEAD_DIM))
    norm_scale = lax.rsqrt(jnp.mean(gated * gated, axis=-1, keepdims=True) + epsilon)
    mixed_heads = (
        (gated * norm_scale * out_gain[which].reshape(head_count, HEAD_DIM))
        .reshape(row_count, inner)
        .astype(jnp.bfloat16)
    )
    return jnp.dot(mixed_heads, w_out[which], preferred_element_type=jnp.float32)


def spread_features(piece):
    return lax.all_gather(piece, "tp", axis=1, tiled=True)


def collect_heads(partial_sum):
    return lax.psum_scatter(
        partial_sum.astype(jnp.bfloat16), "tp", scatter_dimension=1, tiled=True
    ).astype(jnp.float32)


def reorder_rows(stream, col_order):
    count = lax.axis_size(SEQ)
    row_count = stream.shape[0]
    block_rows = row_count // count
    source = col_order // row_count
    local_index = col_order % row_count
    grouping = jnp.argsort(source, stable=True)
    wanted = local_index[grouping].reshape(count, block_rows)
    asked = exchange_by_chip(wanted, (("seq_0", "seq_1"), "seq_2"), (1, 0), 0, 0)
    payload = stream[asked.reshape(-1)].reshape(count, block_rows, stream.shape[1])
    arrived = exchange_by_chip(payload, (("seq_0", "seq_1"), "seq_2"), (1, 0), 0, 0).reshape(
        row_count, stream.shape[1]
    )
    placement = jnp.argsort(grouping)
    return arrived[placement]


def body(
    tokens,
    col_order,
    in_gain,
    w_in,
    w_bc,
    w_dt,
    conv_x,
    conv_bc,
    dt_bias,
    a_log,
    d_skip,
    out_gain,
    w_out,
):
    params = (in_gain, w_in, w_bc, w_dt, conv_x, conv_bc, dt_bias, a_log, d_skip, out_gain, w_out)
    first_full = spread_features(tokens)
    first_part = mixer(first_full, 0, params)
    row_result = (tokens.astype(jnp.float32) + collect_heads(first_part)).astype(jnp.bfloat16)
    own_rows = reorder_rows(row_result, col_order)
    second_full = spread_features(own_rows)
    second_part = mixer(second_full, 1, params)
    return (own_rows.astype(jnp.float32) + collect_heads(second_part)).astype(jnp.bfloat16)


def solution(mesh):
    torus = Mesh(mesh.devices.reshape(4, 4, 2, mesh.shape["tp"]), ("seq_0", "seq_1", "seq_2", "tp"))
    return jax.shard_map(
        body,
        mesh=torus,
        in_specs=(
            P(SEQ, "tp"),
            P(SEQ),
            P(),
            P(None, None, None, "tp"),
            P(),
            P(None, None, "tp"),
            P(None, None, "tp"),
            P(),
            P(None, "tp"),
            P(None, "tp"),
            P(None, "tp"),
            P(None, "tp"),
            P(None, "tp", None),
        ),
        out_specs=P(SEQ, "tp"),
        check_vma=False,
    )
```

profile of v0, /device:TPU:1, one launch (start us, length us, event | category | flops | bytes accessed | tf_op | source)
XLA Modules:
  0.0 575.8 jit_solution(12658820675319592210)
XLA Ops:
  7.3 7.9 %fusion.98 = (bf16[1,2048,2,512]{3,2,1,0:T(2,128)(2,1)}, bf16[1,2048,2,512]{3,2,1,0:T(2,128)(2,1)S(1)}) fusion(bf16[2,2048,2,512]{3,2,1,0:T(2,128)(2,1)} %param.20), kind=kLoop, calls=%fused_computation.187 | loop fusion | bytes 16777216 | tf_op jit(solution)/shard_map/slice | solution.py:99
  15.3 3.2 copy.200
  20.9 39.6 %all-gather.8.cloned.1.call-done = bf16[1024,2048]{1,0:T(8,128)(2,1)} async-done(((bf16[1024,512]{1,0:T(8,128)(2,1)}), bf16[1024,2048]{1,0:T(8,128)(2,1)}) %all-gather.8.cloned.1.call-update) | async-done | bytes 4194320 | tf_op jit(solution)/shard_map/all_gather | solution.py:157
  60.5 3.2 fusion.2
  63.9 7.2 %convolution_convert_fusion.3 = bf16[1024,1024]{1,0:T(8,128)(2,1)S(1)} fusion(bf16[2048,1024]{1,0:T(8,128)(2,1)} %bitcast.229, bf16[1024,2048]{1,0:T(8,128)(2,1)S(1)} %copy-done.14, f32[2048]{0:T(1024)S(1)} %bitcast.255, f32[1024]{0:T(1024)S(1)} %add_rsqrt_fusion.1), kind=kOutput, calls=%fused_computation.92 | convolution fusion | flops 4304404480 | bytes 10498048 | tf_op jit(solution)/shard_map/dot_general | solution.py:98
  75.0 23.3 %fusion.107 = f32[8,128,8]{2,0,1:T(8,128)S(1)} fusion(f32[8,128,8]{2,0,1:T(8,128)S(1)} %copy.146), kind=kOutput, calls=%fused_computation.197 | output fusion | flops 1040384 | bytes 65536 | tf_op jit(solution)/shard_map/jit(cumsum)/reduce_window_sum | solution.py:117
  98.9 3.7 collective-permute-start
  102.6 3.8 convolution_convert_fusion.5
  124.4 3.5 fusion.43
  129.5 19.8 %while.26 = (s32[]{:T(128)}, f32[8,64,128]{2,1,0:T(8,128)S(1)}, f32[8,8,64,128]{3,2,1,0:T(8,128)}, f32[8,8]{1,0:T(8,128)}, f32[8,8,64,128]{3,2,1,0:T(8,128)}, /*index=5*/s32[]{:T(128)}, s32[]{:T(128)}) while((s32[]{:T(128)}, f32[8,64,128]{2,1,0:T(8,128)S(1)}, f32[8,8,64,128]{3,2,1,0:T(8,128)}, f32[8,8]{1,0:T(8,128)}, ...), condition=%wide.region_3.4_spmd.clone, body=%wide.region_2.3_spmd.clone.sunk | while | flops 262147 | bytes 1311424 | solution.py:129
  153.1 7.8 %all-to-all-start = ((f32[32,1,8]{2,1,0:T(1,128)}), f32[32,1,8]{2,1,0:T(1,128)S(1)}, u32[]{:S(2)}, u32[]{:S(2)}) async-start(f32[32,1,8]{2,1,0:T(1,128)} %broadcast_in_dim.64), calls=%async_computation | async-start | bytes 32768 | tf_op jit(solution)/shard_map/all_to_all | solution.py:23
  167.2 4.1 copy.159
  172.9 3.2 fusion.110
  176.1 9.7 %fusion.17 = f32[8,8,64,128]{3,2,1,0:T(8,128)} fusion(f32[8,128,8,64]{1,0,3,2:T(8,128)S(1)} %copy-done.18, f32[8,8,128]{2,1,0:T(8,128)S(1)} %copy.147, f32[8,128,128]{2,1,0:T(8,128)S(1)} %fusion.109, pred[128,128]{1,0:T(8,128)(4,1)S(1)} %iota_compare_fusion), kind=kOutput, calls=%fused_computation.30 | convolution fusion | flops 808452096 | bytes 4767744 | tf_op jit(solution)/shard_map/chqk,ckhp->cqhp/dot_general | solution.py:122
  185.7 11.7 %all-gather.10.cloned.1.call-done = bf16[256,64,128]{2,1,0:T(8,128)(2,1)} async-done(((bf16[8,64,128]{2,1,0:T(8,128)(2,1)}), bf16[256,64,128]{2,1,0:T(8,128)(2,1)}) %all-gather.10.cloned.1.call-update) | async-done | bytes 4194320 | tf_op jit(solution)/shard_map/all_gather | solution.py:82
  197.4 6.2 %fusion.10 = f32[8,1,64,128]{3,1,2,0:T(1,128)S(1)} fusion(f32[32,8,1,1]{0,2,3,1:T(1,128)S(1)} %copy.184, bf16[32,8,64,128]{3,2,1,0:T(8,128)(2,1)} %bitcast.226), kind=kOutput, calls=%fused_computation.23 | convolution fusion | flops 25165824 | bytes 4457472 | tf_op jit(solution)/shard_map/mh,mhpn->hpn/dot_general | solution.py:79
  203.7 5.1 fusion.42
  211.6 4.8 reshape.289
  218.6 8.5 %convolution_convert_fusion.1 = bf16[1024,2048]{1,0:T(8,128)(2,1)} fusion(bf16[2,512,2048]{2,1,0:T(8,128)(2,1)} %param.29, f32[1024,512]{1,0:T(8,128)} %copy.160, f32[1024,512]{1,0:T(8,128)} %reshape.289, f32[1024,512]{1,0:T(8,128)} %divide_multiply_fusion.1, f32[512]{0:T(512)S(1)} %bitcast.267, f32[512]{0:T(512)S(1)} %copy-done.39, ...), kind=kOutput, calls=%fused_computation.36 | convolution fusion | flops 2155347968 | bytes 13635584 | tf_op jit(solution)/shard_map/dot_general | solution.py:153
  227.8 4.4 sort.34
  232.2 4.5 gather_fusion
  238.1 3.6 all_to_all.38
  242.5 11.0 %all_to_all.39 = s32[16,2,1,32]{3,2,1,0:T(1,128)S(1)} all-to-all(s32[16,2,1,32]{3,2,1,0:T(1,128)S(1)} %copy.162), channel_id=1, replica_groups=mesh['seq_0'=4,'seq_1'=4,'seq_2'=2,'tp'=4] {'seq_0','seq_1'}, dimensions={0} | all-to-all | bytes 8192 | tf_op jit(solution)/shard_map/all_to_all | solution.py:46
  254.8 18.2 %reduce-scatter.3.cloned.1.call-done = bf16[1024,512]{1,0:T(8,128)(2,1)} async-done(((bf16[1024,2048]{1,0:T(8,128)(2,1)}), bf16[1024,512]{1,0:T(8,128)(2,1)}) %reduce-scatter.3.cloned.1.call-update) | async-done | bytes 1048592 | tf_op jit(solution)/shard_map/reduce_scatter | solution.py:161
  274.5 4.0 gather_fusion.1
  278.6 4.8 all_to_all.40
  284.5 6.7 %all-to-all-start.4 = ((bf16[16,2,1,32,512]{4,3,1,2,0:T(8,128)(2,1)}), bf16[16,2,1,32,512]{4,3,1,2,0:T(8,128)(2,1)S(1)}, u32[]{:S(2)}, u32[]{:S(2)}) async-start(bf16[16,2,1,32,512]{4,3,1,2,0:T(8,128)(2,1)} %copy.164), calls=%async_computation.5 | async-start | bytes 2097152 | tf_op jit(solution)/shard_map/all_to_all | solution.py:46
  291.2 4.4 sort.35
  295.6 11.9 %all-to-all-done.4 = bf16[16,2,1,32,512]{4,3,1,2,0:T(8,128)(2,1)S(1)} async-done(((bf16[16,2,1,32,512]{4,3,1,2,0:T(8,128)(2,1)}), bf16[16,2,1,32,512]{4,3,1,2,0:T(8,128)(2,1)S(1)}, u32[]{:S(2)}, u32[]{:S(2)}) %all-to-all-start.4) | async-done | bytes 1048608 | tf_op jit(solution)/shard_map/all_to_all | solution.py:46
  307.5 5.1 gather_fusion.2
  312.8 5.5 copy.202
  318.4 39.9 %all-gather.12.cloned.1.call-done = bf16[1024,2048]{1,0:T(8,128)(2,1)} async-done(((bf16[1024,512]{1,0:T(8,128)(2,1)}), bf16[1024,2048]{1,0:T(8,128)(2,1)}) %all-gather.12.cloned.1.call-update) | async-done | bytes 4194320 | tf_op jit(solution)/shard_map/all_gather | solution.py:157
  358.3 3.2 fusion.5
  363.7 3.7 collective-permute-start.3
  369.1 23.3 %fusion.108 = f32[8,128,8]{2,0,1:T(8,128)S(1)} fusion(f32[8,128,8]{2,0,1:T(8,128)S(1)} %copy.167), kind=kOutput, calls=%fused_computation.198 | output fusion | flops 1040384 | bytes 65536 | tf_op jit(solution)/shard_map/jit(cumsum)/reduce_window_sum | solution.py:117
  392.5 8.0 %convolution_convert_fusion.2 = bf16[1024,1024]{1,0:T(8,128)(2,1)S(1)} fusion(bf16[2048,1024]{1,0:T(8,128)(2,1)} %bitcast.230, bf16[1024,2048]{1,0:T(8,128)(2,1)} %all-gather.12.cloned.1.call-done, f32[2048]{0:T(1024)S(1)} %bitcast.254, f32[1024]{0:T(1024)S(1)} %add_rsqrt_fusion), kind=kOutput, calls=%fused_computation.91 | convolution fusion | flops 4304404480 | bytes 10498048 | tf_op jit(solution)/shard_map/dot_general | solution.py:98
  418.7 3.5 fusion.36
  423.8 19.8 %while.27 = (s32[]{:T(128)}, f32[8,64,128]{2,1,0:T(8,128)S(1)}, f32[8,8,64,128]{3,2,1,0:T(8,128)}, f32[8,8]{1,0:T(8,128)}, f32[8,8,64,128]{3,2,1,0:T(8,128)}, /*index=5*/s32[]{:T(128)}, s32[]{:T(128)}) while((s32[]{:T(128)}, f32[8,64,128]{2,1,0:T(8,128)S(1)}, f32[8,8,64,128]{3,2,1,0:T(8,128)}, f32[8,8]{1,0:T(8,128)}, ...), condition=%wide.region_15.16_spmd.clone, body=%wide.region_14.15_spmd.clone.sunk | while | flops 262147 | bytes 1311424 | solution.py:129
  445.1 7.2 %all-to-all-start.5 = ((f32[32,1,8]{2,1,0:T(1,128)}), f32[32,1,8]{2,1,0:T(1,128)S(1)}, u32[]{:S(2)}, u32[]{:S(2)}) async-start(f32[32,1,8]{2,1,0:T(1,128)} %broadcast_in_dim.112), calls=%async_computation.6 | async-start | bytes 32768 | tf_op jit(solution)/shard_map/all_to_all | solution.py:23
  458.6 4.3 copy.180
  464.5 3.2 fusion.112
  467.7 9.7 %fusion.12 = f32[8,8,64,128]{3,2,1,0:T(8,128)} fusion(f32[8,128,8,64]{1,0,3,2:T(8,128)S(1)} %copy-done.19, f32[8,8,128]{2,1,0:T(8,128)S(1)} %copy.168, f32[8,128,128]{2,1,0:T(8,128)S(1)} %fusion.111, pred[128,128]{1,0:T(8,128)(4,1)S(1)} %iota_compare_fusion), kind=kOutput, calls=%fused_computation.25 | convolution fusion | flops 808452096 | bytes 4767744 | tf_op jit(solution)/shard_map/chqk,ckhp->cqhp/dot_general | solution.py:122
  477.4 13.8 %all-gather.14.cloned.1.call-done = bf16[256,64,128]{2,1,0:T(8,128)(2,1)} async-done(((bf16[8,64,128]{2,1,0:T(8,128)(2,1)}), bf16[256,64,128]{2,1,0:T(8,128)(2,1)}) %all-gather.14.cloned.1.call-update) | async-done | bytes 4194320 | tf_op jit(solution)/shard_map/all_gather | solution.py:82
  491.1 6.0 %fusion.8 = f32[8,1,64,128]{3,1,2,0:T(1,128)S(1)} fusion(f32[32,8,1,1]{0,2,3,1:T(1,128)S(1)} %copy.189, bf16[32,8,64,128]{3,2,1,0:T(8,128)(2,1)} %bitcast.227), kind=kOutput, calls=%fused_computation.21 | convolution fusion | flops 25165824 | bytes 4457472 | tf_op jit(solution)/shard_map/mh,mhpn->hpn/dot_general | solution.py:79
  497.2 5.1 fusion.35
  505.0 4.8 reshape.290
  512.0 8.4 %convolution_convert_fusion = bf16[1024,2048]{1,0:T(8,128)(2,1)} fusion(bf16[2,512,2048]{2,1,0:T(8,128)(2,1)} %param.29, f32[1024,512]{1,0:T(8,128)} %copy.181, f32[1024,512]{1,0:T(8,128)} %reshape.290, f32[1024,512]{1,0:T(8,128)} %divide_multiply_fusion, f32[512]{0:T(512)S(1)} %bitcast.266, f32[512]{0:T(512)S(1)} %mul.565, bf16[1024,1024]{1,0:T(8,128)(2,1)} %copy-done.17), kind=kOutput, calls=%fused_computation.35 | convolution fusion | flops 2155347968 | bytes 13635584 | tf_op jit(solution)/shard_map/dot_general | solution.py:153
  520.5 45.8 %reduce-scatter.5.cloned.1.call-done = bf16[1024,512]{1,0:T(8,128)(2,1)} async-done(((bf16[1024,2048]{1,0:T(8,128)(2,1)}), bf16[1024,512]{1,0:T(8,128)(2,1)}) %reduce-scatter.5.cloned.1.call-update) | async-done | bytes 1048592 | tf_op jit(solution)/shard_map/reduce_scatter | solution.py:161
  (290 shorter events, 130.4 us)
Async XLA Ops:
  6.5 53.9 %all-gather.8.cloned.1.call-start = ((), (), s32[]{:S(2)}) async-start(), calls=%async_computation.8 | async-start | bytes 5242880 | tf_op jit(solution)/shard_map/all_gather | solution.py:157
  7.3 190.2 %all-gather.10.cloned.1.call-start = ((), (), s32[]{:S(2)}) async-start(), calls=%async_computation.11 | async-start | bytes 4325376 | tf_op jit(solution)/shard_map/all_gather | solution.py:82
  15.3 3.2 copy-start.45
  15.3 3.8 copy-start.46
  15.3 4.4 copy-start.28
  15.3 5.0 copy-start.24
  15.3 5.0 copy-start.25
  60.5 3.4 copy-start.14
  98.9 15.1 %collective-permute-start = (bf16[3,512]{1,0:T(4,128)(2,1)}, bf16[3,512]{1,0:T(4,128)(2,1)S(1)}, u32[]{:S(2)}, u32[]{:S(2)}) collective-permute-start(bf16[3,512]{1,0:T(4,128)(2,1)} %slice.314), channel_id=1, source_target_pairs={{0,4},{4,8},{8,12},{12,16},{16,20},{20,24},{24,28},{28,32},{32,36}... | collective-permute-start | bytes 9224 | tf_op jit(solution)/shard_map/ppermute | solution.py:33
  106.4 5.4 copy-start.34
  106.4 5.4 copy-start.35
  107.3 3.4 collective-permute-start.1
  129.5 20.5 %copy-start.47 = (f32[2,8]{1,0:T(2,128)S(1)}, f32[2,8]{1,0:T(2,128)}, u32[]{:S(2)}) copy-start(f32[2,8]{1,0:T(2,128)} %param.27) | copy-start | bytes 196
  129.5 22.3 %copy-start.37 = (f32[2,512]{1,0:T(2,128)S(1)}, f32[2,512]{1,0:T(2,128)}, u32[]{:S(2)}) copy-start(f32[2,512]{1,0:T(2,128)} %param.28) | copy-start | bytes 12292
  153.1 18.2 %all-to-all-start = ((f32[32,1,8]{2,1,0:T(1,128)}), f32[32,1,8]{2,1,0:T(1,128)S(1)}, u32[]{:S(2)}, u32[]{:S(2)}) async-start(f32[32,1,8]{2,1,0:T(1,128)} %broadcast_in_dim.64), calls=%async_computation | async-start | bytes 32768 | tf_op jit(solution)/shard_map/all_to_all | solution.py:23
  160.9 112.1 %reduce-scatter.3.cloned.1.call-start = ((), (), s32[]{:S(2)}) async-start(), calls=%async_computation.9 | async-start | bytes 5242880 | tf_op jit(solution)/shard_map/reduce_scatter | solution.py:161
  167.2 4.2 copy-start.26
  167.2 4.5 copy-start.8
  167.2 5.7 copy-start.5
  172.9 3.2 copy-start.18
  197.4 6.3 %copy-start.2 = (f32[64,8,8,128]{3,2,1,0:T(8,128)S(1)}, f32[64,8,8,128]{3,2,1,0:T(8,128)}, u32[]{:S(2)}) copy-start(f32[64,8,8,128]{3,2,1,0:T(8,128)} %copy-done.1) | copy-start | bytes 6291460
  197.4 6.3 %copy-start.21 = (f32[8,128,8,64]{1,3,2,0:T(8,128)S(1)}, f32[8,128,8,64]{1,3,2,0:T(8,128)}, u32[]{:S(2)}) copy-start(f32[8,128,8,64]{1,3,2,0:T(8,128)} %copy.159) | copy-start | bytes 6291460
  197.4 6.3 %copy-start.42 = (f32[8]{0:T(128)S(1)}, f32[8]{0:T(128)}, u32[]{:S(2)}) copy-start(f32[8]{0:T(128)} %copy-done.41) | copy-start | bytes 100
  232.2 40.8 %copy-start.11 = (bf16[1024,512]{1,0:T(8,128)(2,1)S(1)}, bf16[1024,512]{1,0:T(8,128)(2,1)}, u32[]{:S(2)}) copy-start(bf16[1024,512]{1,0:T(8,128)(2,1)} %param.17) | copy-start | bytes 3145732
  284.5 23.0 %all-to-all-start.4 = ((bf16[16,2,1,32,512]{4,3,1,2,0:T(8,128)(2,1)}), bf16[16,2,1,32,512]{4,3,1,2,0:T(8,128)(2,1)S(1)}, u32[]{:S(2)}, u32[]{:S(2)}) async-start(bf16[16,2,1,32,512]{4,3,1,2,0:T(8,128)(2,1)} %copy.164), calls=%async_computation.5 | async-start | bytes 2097152 | tf_op jit(solution)/shard_map/all_to_all | solution.py:46
  291.2 67.1 %all-gather.12.cloned.1.call-start = ((), (), s32[]{:S(2)}) async-start(), calls=%async_computation.12 | async-start | bytes 5242880 | tf_op jit(solution)/shard_map/all_gather | solution.py:157
  312.6 178.5 %all-gather.14.cloned.1.call-start = ((), (), s32[]{:S(2)}) async-start(), calls=%async_computation.13 | async-start | bytes 4325376 | tf_op jit(solution)/shard_map/all_gather | solution.py:82
  312.8 48.7 %copy-start.49 = (bf16[2,2048,256]{2,1,0:T(8,128)(2,1)S(1)}, bf16[2,2048,256]{2,1,0:T(8,128)(2,1)}, u32[]{:S(2)}) copy-start(bf16[2,2048,256]{2,1,0:T(8,128)(2,1)} %param.21) | copy-start | bytes 6291460
  318.4 43.2 %copy-start.29 = (f32[1,2048]{1,0:T(1,128)S(1)}, f32[1,2048]{1,0:T(1,128)}, u32[]{:S(2)}) copy-start(f32[1,2048]{1,0:T(1,128)} %get-tuple-element.155) | copy-start | bytes 24580
  358.3 3.4 copy-start.15
  361.8 5.7 copy-start.48
  361.8 5.7 copy-start.51
  363.1 5.7 copy-start.22
  363.7 41.9 %collective-permute-start.3 = (bf16[3,256]{1,0:T(4,128)(2,1)}, bf16[3,256]{1,0:T(4,128)(2,1)}, u32[]{:S(2)}, u32[]{:S(2)}) collective-permute-start(bf16[3,256]{1,0:T(4,128)(2,1)} %slice.336), channel_id=1, source_target_pairs={{0,4},{4,8},{8,12},{12,16},{16,20},{20,24},{24,28},{28,32},{32,36}... | collective-permute-start | bytes 4616 | tf_op jit(solution)/shard_map/ppermute | solution.py:33
  402.0 4.7 copy-start.30
  402.0 4.8 copy-start.31
  402.0 4.8 copy-start.32
  402.0 4.8 copy-start.33
  403.4 4.9 collective-permute-start.2
  423.8 20.5 %copy-start.40 = (f32[8]{0:T(128)S(1)}, f32[8]{0:T(128)}, u32[]{:S(2)}) copy-start(f32[8]{0:T(128)} %get-tuple-element.169) | copy-start | bytes 100
  445.1 17.9 %all-to-all-start.5 = ((f32[32,1,8]{2,1,0:T(1,128)}), f32[32,1,8]{2,1,0:T(1,128)S(1)}, u32[]{:S(2)}, u32[]{:S(2)}) async-start(f32[32,1,8]{2,1,0:T(1,128)} %broadcast_in_dim.112), calls=%async_computation.6 | async-start | bytes 32768 | tf_op jit(solution)/shard_map/all_to_all | solution.py:23
  452.3 114.0 %reduce-scatter.5.cloned.1.call-start = ((), (), s32[]{:S(2)}) async-start(), calls=%async_computation.10 | async-start | bytes 5242880 | tf_op jit(solution)/shard_map/reduce_scatter | solution.py:161
  458.6 4.4 copy-start.27
  458.6 4.7 copy-start.10
  458.6 5.9 %copy-start.6 = (f32[8,8,64,128]{3,2,1,0:T(8,128)S(1)}, f32[8,8,64,128]{3,2,1,0:T(8,128)}, u32[]{:S(2)}) copy-start(f32[8,8,64,128]{3,2,1,0:T(8,128)} %get-tuple-element.67) | copy-start | bytes 6291460
  491.1 6.0 %copy-start.4 = (f32[64,8,8,128]{3,2,1,0:T(8,128)S(1)}, f32[64,8,8,128]{3,2,1,0:T(8,128)}, u32[]{:S(2)}) copy-start(f32[64,8,8,128]{3,2,1,0:T(8,128)} %copy-done.3) | copy-start | bytes 6291460
  491.1 6.0 %copy-start.20 = (f32[8,128,8,64]{1,3,2,0:T(8,128)S(1)}, f32[8,128,8,64]{1,3,2,0:T(8,128)}, u32[]{:S(2)}) copy-start(f32[8,128,8,64]{1,3,2,0:T(8,128)} %copy.180) | copy-start | bytes 6291460
  520.5 45.9 %copy-start = (bf16[1024,512]{1,0:T(8,128)(2,1)S(1)}, bf16[1024,512]{1,0:T(8,128)(2,1)}, u32[]{:S(2)}) copy-start(bf16[1024,512]{1,0:T(8,128)(2,1)} %gather_fusion.2) | copy-start | bytes 3145732
  (17 other events, 31.2 us)
Sparse Core Ops, SparseCore 0:
  9.0 51.3 all-gather.7
  150.1 47.2 all-gather.9
  227.2 45.7 reduce-scatter.2
  312.7 45.5 all-gather.11
  444.4 46.7 all-gather.13
  520.6 45.6 reduce-scatter.4
where the time goes:
time: 584 us; the launch traced here: 576 us
  waiting for transfers between devices  183 us (31%)
  other arithmetic  118 us (20%)
  local copies, waits for them, and re-layouts  110 us (19%)
  matrix products  97.5 us (17%)
  starting transfers between devices  33.7 us (6%)
  blocking collectives  19.4 us (3%)
  between operations  14.5 us (2%)
    all_gather x2, waiting for transfers between devices, spread_features(): return lax.all_gather(piece, 'tp', axis=1, tiled=True)  79.5 us
    reduce_scatter x2, waiting for transfers between devices, collect_heads(): lax.psum_scatter(partial_sum.astype(jnp.bfloat16), 'tp', scatter_dimensio...  64.1 us
    another operation x2, other arithmetic, mixer(): cumul = jnp.cumsum(log_blocks, axis=1)  46.6 us
    all_gather x2, waiting for transfers between devices, incoming_state(): lax.all_gather(local_end[None].astype(jnp.bfloat16), SEQ, axis=0, tiled=T...  25.5 us
    all_to_all x3, blocking collectives, moved_by_axis(): lax.all_to_all(blocks, axes[k], split_axis=k, concat_axis=k, tiled=True)  19.4 us
    dot_general x2, matrix products, mixer(): jnp.einsum('chqk,ckhp->cqhp', intersection[:, None] * jnp.exp(spread), fe...  19.3 us
    dot_general x2, matrix products, mixer(): jnp.dot(mixed_heads, w_out[which], preferred_element_type=jnp.float32)  17 us
    unnamed x111, local copies, waits for them, and re-layouts  16.7 us
  transfers between devices with their start and end apart: 13, of which 8 were waited for; matrix products, arithmetic and copies ran while one was open for 24% of the time, Pallas kernels for 0%

commit v1 on v0

--- a/solution.py
+++ b/solution.py
@@ -10,6 +10,19 @@
 SEQ = ("seq_0", "seq_1", "seq_2")
 highest = lax.Precision.HIGHEST
 epsilon = 1e-05
+
+
+def gather_around(shard, axis, dim):
+    ways = lax.axis_size(axis)
+    up = [(d, (d + 1) % ways) for d in range(ways)]
+    down = [(d, (d - 1) % ways) for d in range(ways)]
+    earlier, later = ([shard], [shard])
+    for _ in range(ways // 2):
+        earlier.append(lax.ppermute(earlier[-1], axis, up))
+    for _ in range((ways - 1) // 2):
+        later.append(lax.ppermute(later[-1], axis, down))
+    line = jnp.concatenate([*earlier[::-1], *later[1:]], axis=dim)
+    return jnp.roll(line, (lax.axis_index(axis) - ways // 2) * shard.shape[dim], axis=dim)
 
 
 def laid_out(blocks, dim):
@@ -154,7 +167,7 @@
 
 
 def spread_features(piece):
-    return lax.all_gather(piece, "tp", axis=1, tiled=True)
+    return gather_around(piece, "tp", 1)
 
 
 def collect_heads(partial_sum):

time: 584 us -> 592 us (1.014)
  waiting for transfers between devices: 183 us -> 166 us
  other arithmetic: 118 us -> 133 us
  starting transfers between devices: 33.7 us -> 45.1 us
    all_gather x2 -> x0, waiting for transfers between devices: 79.5 us -> none  [spread_features(): return lax.all_gather(piece, 'tp', axis=1, tiled=True)]
    ppermute x0 -> x6, waiting for transfers between devices: none -> 71.5 us  [the longest x4 71.5 us: gather_around(): earlier.append(lax.ppermute(earlier[-1], axis, up))]
    reduce_sum x2, other arithmetic: 6.44 us -> 21.9 us  [mixer(): scale = lax.rsqrt(jnp.mean(widen * widen, axis=-1, keepdims=True) + epsilon)]
    all_gather x2, waiting for transfers between devices: 25.5 us -> 18.9 us  [incoming_state(): lax.all_gather(local_end[None].astype(jnp.bfloat16), SEQ, axis=0, tiled=T...]
    ppermute x0 -> x6, starting transfers between devices: none -> 6.53 us  [the longest x2 3.93 us: gather_around(): later.append(lax.ppermute(later[-1], axis, down))]
    unnamed x111 -> x101, local copies, waits for them, and re-layouts: 16.7 us -> 16.4 us
  transfers between devices with their start and end apart: 13 -> 17, of which waited for: 8 -> 9; matrix products, arithmetic and copies ran while one was open for 24% -> 23% of each run, Pallas kernels for 0% -> 0%
where the time goes in v1:
time: 592 us; the launch traced here: 582 us
  waiting for transfers between devices  166 us (28%)
  other arithmetic  133 us (22%)
  local copies, waits for them, and re-layouts  106 us (18%)
  matrix products  98.2 us (17%)
  starting transfers between devices  45.1 us (8%)
  blocking collectives  19.4 us (3%)
  between operations  14.2 us (2%)
    ppermute x4, waiting for transfers between devices, gather_around(): earlier.append(lax.ppermute(earlier[-1], axis, up))  71.5 us
    reduce_scatter x2, waiting for transfers between devices, collect_heads(): lax.psum_scatter(partial_sum.astype(jnp.bfloat16), 'tp', scatter_dimensio...  63.6 us
    another operation x2, other arithmetic, mixer(): cumul = jnp.cumsum(log_blocks, axis=1)  46.6 us
    reduce_sum x2, other arithmetic, mixer(): scale = lax.rsqrt(jnp.mean(widen * widen, axis=-1, keepdims=True) + epsilon)  21.9 us
    all_to_all x3, blocking collectives, moved_by_axis(): lax.all_to_all(blocks, axes[k], split_axis=k, concat_axis=k, tiled=True)  19.4 us
    dot_general x2, matrix products, mixer(): jnp.einsum('chqk,ckhp->cqhp', intersection[:, None] * jnp.exp(spread), fe...  19.3 us
    all_gather x2, waiting for transfers between devices, incoming_state(): lax.all_gather(local_end[None].astype(jnp.bfloat16), SEQ, axis=0, tiled=T...  18.9 us
    dot_general x2, matrix products, mixer(): jnp.dot(mixed_heads, w_out[which], preferred_element_type=jnp.float32)  16.9 us
  transfers between devices with their start and end apart: 17, of which 9 were waited for; matrix products, arithmetic and copies ran while one was open for 23% of the time, Pallas kernels for 0%

profile of v1, /device:TPU:1, one launch (start us, length us, event | category | flops | bytes accessed | tf_op | source)
XLA Modules:
  0.0 582.1 jit_solution(9972186400385697491)
XLA Ops:
  9.8 7.9 %fusion.114 = (bf16[1,2048,2,512]{3,2,1,0:T(2,128)(2,1)}, bf16[1,2048,2,512]{3,2,1,0:T(2,128)(2,1)S(1)}) fusion(bf16[2,2048,2,512]{3,2,1,0:T(2,128)(2,1)} %param.22), kind=kLoop, calls=%fused_computation.217 | loop fusion | bytes 16777216 | tf_op jit(solution)/shard_map/slice | solution.py:112
  21.6 10.9 %collective-permute-done = bf16[1024,512]{1,0:T(8,128)(2,1)S(1)} collective-permute-done((bf16[1024,512]{1,0:T(8,128)(2,1)}, bf16[1024,512]{1,0:T(8,128)(2,1)S(1)}, u32[]{:S(2)}, u32[]{:S(2)}) %collective-permute-start) | collective-permute-done | bytes 1048608 | tf_op jit(solution)/shard_map/ppermute | solution.py:21
  34.6 22.1 %collective-permute-done.1 = bf16[1024,512]{1,0:T(8,128)(2,1)S(1)} collective-permute-done((bf16[1024,512]{1,0:T(8,128)(2,1)S(1)}, bf16[1024,512]{1,0:T(8,128)(2,1)S(1)}, u32[]{:S(2)}, u32[]{:S(2)}) %collective-permute-start.1) | collective-permute-done | bytes 1048608 | tf_op jit(solution)/shard_map/ppermute | solution.py:21
  56.7 11.5 %fusion.2 = (f32[1024]{0:T(1024)S(1)}, bf16[1024,2048]{1,0:T(8,128)(2,1)S(1)}) fusion(s32[]{:T(128)S(6)} %select_n.80, bf16[1024,512]{1,0:T(8,128)(2,1)S(1)} %collective-permute-done.2, bf16[1024,512]{1,0:T(8,128)(2,1)S(1)} %copy-done.12, bf16[1024,512]{1,0:T(8,128)(2,1)S(1)} %collective-permute-done, bf16[1024,512]{1,0:T(8,128)(2,1)S(1)} %collective-permute-done.1), kind=kLoop, calls=%fused_computation.15 | loop fusion | flops 39844864 | bytes 8392708 | tf_op jit(solution)/shard_map/reduce_sum | solution.py:109
  68.2 4.9 convolution_convert_fusion.3
  77.0 23.3 %fusion.123 = f32[8,128,8]{2,0,1:T(8,128)S(1)} fusion(f32[8,128,8]{2,0,1:T(8,128)S(1)} %copy.146), kind=kOutput, calls=%fused_computation.227 | output fusion | flops 1040384 | bytes 65536 | tf_op jit(solution)/shard_map/jit(cumsum)/reduce_window_sum | solution.py:130
  100.9 3.8 convolution_convert_fusion.5
  105.3 6.0 %collective-permute-start.4 = (bf16[3,256]{1,0:T(4,128)(2,1)}, bf16[3,256]{1,0:T(4,128)(2,1)}, u32[]{:S(2)}, u32[]{:S(2)}) collective-permute-start(bf16[3,256]{1,0:T(4,128)(2,1)} %slice.320), channel_id=1, source_target_pairs={{0,4},{4,8},{8,12},{12,16},{16,20},{20,24},{24,28},{28,32},{32,36}... | collective-permute-start | bytes 4616 | tf_op jit(solution)/shard_map/ppermute | solution.py:46
  132.7 19.7 %while.26 = (s32[]{:T(128)}, f32[8,64,128]{2,1,0:T(8,128)S(1)}, f32[8,8,64,128]{3,2,1,0:T(8,128)}, f32[8,8]{1,0:T(8,128)}, f32[8,8,64,128]{3,2,1,0:T(8,128)}, /*index=5*/s32[]{:T(128)}, s32[]{:T(128)}) while((s32[]{:T(128)}, f32[8,64,128]{2,1,0:T(8,128)S(1)}, f32[8,8,64,128]{3,2,1,0:T(8,128)}, f32[8,8]{1,0:T(8,128)}, ...), condition=%wide.region_3.5_spmd.clone, body=%wide.region_2.4_spmd.clone.sunk | while | flops 262147 | bytes 1311424 | solution.py:142
  156.3 8.3 %all-to-all-start = ((f32[32,1,8]{2,1,0:T(1,128)}), f32[32,1,8]{2,1,0:T(1,128)S(1)}, u32[]{:S(2)}, u32[]{:S(2)}) async-start(f32[32,1,8]{2,1,0:T(1,128)} %broadcast_in_dim.64), calls=%async_computation | async-start | bytes 32768 | tf_op jit(solution)/shard_map/all_to_all | solution.py:36
  170.9 4.2 copy.159
  179.8 9.6 %fusion.31 = f32[8,8,64,128]{3,2,1,0:T(8,128)} fusion(f32[8,128,8,64]{1,0,3,2:T(8,128)S(1)} %copy-done.16, f32[8,8,128]{2,1,0:T(8,128)S(1)} %copy.147, f32[8,128,128]{2,1,0:T(8,128)S(1)} %fusion.125, pred[128,128]{1,0:T(8,128)(4,1)S(1)} %iota_compare_fusion), kind=kOutput, calls=%fused_computation.60 | convolution fusion | flops 808452096 | bytes 4767744 | tf_op jit(solution)/shard_map/chqk,ckhp->cqhp/dot_general | solution.py:135
  189.4 10.2 %all-gather.5.cloned.1.call-done = bf16[256,64,128]{2,1,0:T(8,128)(2,1)} async-done(((bf16[8,64,128]{2,1,0:T(8,128)(2,1)}), bf16[256,64,128]{2,1,0:T(8,128)(2,1)}) %all-gather.5.cloned.1.call-update) | async-done | bytes 4194320 | tf_op jit(solution)/shard_map/all_gather | solution.py:95
  199.6 6.2 %fusion.24 = f32[8,1,64,128]{3,1,2,0:T(1,128)S(1)} fusion(f32[32,8,1,1]{0,2,3,1:T(1,128)S(1)} %copy.184, bf16[32,8,64,128]{3,2,1,0:T(8,128)(2,1)} %bitcast.226), kind=kOutput, calls=%fused_computation.53 | convolution fusion | flops 25165824 | bytes 4457472 | tf_op jit(solution)/shard_map/mh,mhpn->hpn/dot_general | solution.py:92
  205.9 5.1 fusion.56
  213.8 4.8 reshape.288
  220.8 8.5 %convolution_convert_fusion.1 = bf16[1024,2048]{1,0:T(8,128)(2,1)} fusion(bf16[2,512,2048]{2,1,0:T(8,128)(2,1)} %param.31, f32[1024,512]{1,0:T(8,128)} %copy.160, f32[1024,512]{1,0:T(8,128)} %reshape.288, f32[1024,512]{1,0:T(8,128)} %divide_multiply_fusion.1, f32[512]{0:T(512)S(1)} %bitcast.267, f32[512]{0:T(512)S(1)} %copy-done.34, ...), kind=kOutput, calls=%fused_computation.66 | convolution fusion | flops 2155347968 | bytes 13635584 | tf_op jit(solution)/shard_map/dot_general | solution.py:166
  230.0 4.4 sort.34
  234.4 4.5 gather_fusion
  240.3 3.6 all_to_all.38
  244.7 10.9 %all_to_all.39 = s32[16,2,1,32]{3,2,1,0:T(1,128)S(1)} all-to-all(s32[16,2,1,32]{3,2,1,0:T(1,128)S(1)} %copy.162), channel_id=1, replica_groups=mesh['seq_0'=4,'seq_1'=4,'seq_2'=2,'tp'=4] {'seq_0','seq_1'}, dimensions={0} | all-to-all | bytes 8192 | tf_op jit(solution)/shard_map/all_to_all | solution.py:59
  256.9 18.0 %reduce-scatter.3.cloned.1.call-done = bf16[1024,512]{1,0:T(8,128)(2,1)} async-done(((bf16[1024,2048]{1,0:T(8,128)(2,1)}), bf16[1024,512]{1,0:T(8,128)(2,1)}) %reduce-scatter.3.cloned.1.call-update) | async-done | bytes 1048592 | tf_op jit(solution)/shard_map/reduce_scatter | solution.py:174
  276.4 4.0 gather_fusion.1
  280.5 4.8 all_to_all.40
  286.4 6.7 %all-to-all-start.4 = ((bf16[16,2,1,32,512]{4,3,1,2,0:T(8,128)(2,1)}), bf16[16,2,1,32,512]{4,3,1,2,0:T(8,128)(2,1)S(1)}, u32[]{:S(2)}, u32[]{:S(2)}) async-start(bf16[16,2,1,32,512]{4,3,1,2,0:T(8,128)(2,1)} %copy.164), calls=%async_computation.5 | async-start | bytes 2097152 | tf_op jit(solution)/shard_map/all_to_all | solution.py:59
  293.2 4.4 sort.35
  297.5 11.9 %all-to-all-done.4 = bf16[16,2,1,32,512]{4,3,1,2,0:T(8,128)(2,1)S(1)} async-done(((bf16[16,2,1,32,512]{4,3,1,2,0:T(8,128)(2,1)}), bf16[16,2,1,32,512]{4,3,1,2,0:T(8,128)(2,1)S(1)}, u32[]{:S(2)}, u32[]{:S(2)}) %all-to-all-start.4) | async-done | bytes 1048608 | tf_op jit(solution)/shard_map/all_to_all | solution.py:59
  309.4 4.0 gather_fusion.2
  316.1 21.1 %collective-permute-done.5 = bf16[1024,512]{1,0:T(8,128)(2,1)S(1)} collective-permute-done((bf16[1024,512]{1,0:T(8,128)(2,1)S(1)}, bf16[1024,512]{1,0:T(8,128)(2,1)S(1)}, u32[]{:S(2)}, u32[]{:S(2)}) %collective-permute-start.5) | collective-permute-done | bytes 1048608 | tf_op jit(solution)/shard_map/ppermute | solution.py:21
  337.4 5.4 copy.202
  342.8 17.5 %collective-permute-done.6 = bf16[1024,512]{1,0:T(8,128)(2,1)} collective-permute-done((bf16[1024,512]{1,0:T(8,128)(2,1)S(1)}, bf16[1024,512]{1,0:T(8,128)(2,1)}, u32[]{:S(2)}, u32[]{:S(2)}) %collective-permute-start.6) | collective-permute-done | bytes 1048608 | tf_op jit(solution)/shard_map/ppermute | solution.py:21
  360.3 10.4 %fusion.5 = (f32[1024]{0:T(1024)S(1)}, bf16[1024,2048]{1,0:T(8,128)(2,1)S(1)}) fusion(s32[]{:T(128)S(6)} %select_n.80, bf16[1024,512]{1,0:T(8,128)(2,1)} %collective-permute-done.7, bf16[1024,512]{1,0:T(8,128)(2,1)S(1)} %gather_fusion.2, bf16[1024,512]{1,0:T(8,128)(2,1)S(1)} %collective-permute-done.5, bf16[1024,512]{1,0:T(8,128)(2,1)} %collective-permute-done.6), kind=kLoop, calls=%fused_computation.18 | loop fusion | flops 39844864 | bytes 8392708 | tf_op jit(solution)/shard_map/reduce_sum | solution.py:109
  372.1 6.4 %collective-permute-start.9 = (bf16[3,256]{1,0:T(4,128)(2,1)S(1)}, bf16[3,256]{1,0:T(4,128)(2,1)S(1)}, u32[]{:S(2)}, u32[]{:S(2)}) collective-permute-start(bf16[3,256]{1,0:T(4,128)(2,1)S(1)} %slice.336), channel_id=1, source_target_pairs={{0,4},{4,8},{8,12},{12,16},{16,20},{20,24},{24,28},{28,32},{32,36}... | collective-permute-start | bytes 4616 | tf_op jit(solution)/shard_map/ppermute | solution.py:46
  380.1 23.3 %fusion.124 = f32[8,128,8]{2,0,1:T(8,128)S(1)} fusion(f32[8,128,8]{2,0,1:T(8,128)S(1)} %copy.167), kind=kOutput, calls=%fused_computation.228 | output fusion | flops 1040384 | bytes 65536 | tf_op jit(solution)/shard_map/jit(cumsum)/reduce_window_sum | solution.py:130
  403.5 8.0 %convolution_convert_fusion.2 = bf16[1024,1024]{1,0:T(8,128)(2,1)S(1)} fusion(bf16[2048,1024]{1,0:T(8,128)(2,1)} %bitcast.230, bf16[1024,2048]{1,0:T(8,128)(2,1)} %copy-done.10, f32[2048]{0:T(1024)S(1)} %bitcast.254, f32[1024]{0:T(1024)S(1)} %add_rsqrt_fusion), kind=kOutput, calls=%fused_computation.121 | convolution fusion | flops 4304404480 | bytes 10498048 | tf_op jit(solution)/shard_map/dot_general | solution.py:111
  433.2 14.3 %while.27 = (s32[]{:T(128)}, f32[8,64,128]{2,1,0:T(8,128)S(1)}, f32[8,8,64,128]{3,2,1,0:T(8,128)}, f32[8,8]{1,0:T(8,128)S(1)}, f32[8,8,64,128]{3,2,1,0:T(8,128)}, /*index=5*/s32[]{:T(128)}, s32[]{:T(128)}) while((s32[]{:T(128)}, f32[8,64,128]{2,1,0:T(8,128)S(1)}, f32[8,8,64,128]{3,2,1,0:T(8,128)}, f32[8,8]{1,0:T(8,128)S(1)}, ...), condition=%wide.region_15.17_spmd.clone, body=%wide.region_14.16_spmd.clone.sunk | while | flops 262147 | bytes 1311424 | solution.py:142
  449.0 6.8 %all-to-all-start.5 = ((f32[32,1,8]{2,1,0:T(1,128)}), f32[32,1,8]{2,1,0:T(1,128)S(1)}, u32[]{:S(2)}, u32[]{:S(2)}) async-start(f32[32,1,8]{2,1,0:T(1,128)} %broadcast_in_dim.112), calls=%async_computation.6 | async-start | bytes 32768 | tf_op jit(solution)/shard_map/all_to_all | solution.py:36
  459.6 4.5 reshape.291
  464.1 4.2 copy.180
  469.9 4.9 fusion.128
  474.8 9.7 %fusion.26 = f32[8,8,64,128]{3,2,1,0:T(8,128)} fusion(f32[8,128,8,64]{1,0,3,2:T(8,128)S(1)} %copy-done.17, f32[8,8,128]{2,1,0:T(8,128)S(1)} %copy.168, f32[8,128,128]{2,1,0:T(8,128)S(1)} %fusion.127, pred[128,128]{1,0:T(8,128)(4,1)S(1)} %iota_compare_fusion), kind=kOutput, calls=%fused_computation.55 | convolution fusion | flops 808452096 | bytes 4767744 | tf_op jit(solution)/shard_map/chqk,ckhp->cqhp/dot_general | solution.py:135
  484.5 8.7 %all-gather.7.cloned.1.call-done = bf16[256,64,128]{2,1,0:T(8,128)(2,1)} async-done(((bf16[8,64,128]{2,1,0:T(8,128)(2,1)}), bf16[256,64,128]{2,1,0:T(8,128)(2,1)}) %all-gather.7.cloned.1.call-update) | async-done | bytes 4194320 | tf_op jit(solution)/shard_map/all_gather | solution.py:95
  493.2 6.0 %fusion.22 = f32[8,1,64,128]{3,1,2,0:T(1,128)S(1)} fusion(f32[32,8,1,1]{0,2,3,1:T(1,128)S(1)} %copy.189, bf16[32,8,64,128]{3,2,1,0:T(8,128)(2,1)} %bitcast.227), kind=kOutput, calls=%fused_computation.51 | convolution fusion | flops 25165824 | bytes 4457472 | tf_op jit(solution)/shard_map/mh,mhpn->hpn/dot_general | solution.py:92
  499.2 6.5 %fusion.49 = (f32[8,128,8]{1,2,0:T(8,128)S(1)}, f32[8,128,8,64]{1,3,2,0:T(8,128)}) fusion(f32[8,128,8,64]{1,0,3,2:T(8,128)S(1)} %bitcast.211, f32[8,128,8,64]{1,3,2,0:T(8,128)S(1)} %copy-done.18, f32[8]{0:T(128)S(1)} %copy-done.35, f32[8,128,8]{1,2,0:T(8,128)S(1)} %copy.174, f32[8,128,128,1]{2,1,3,0:T(8,128)S(1)} %bitcast.223, ...), kind=kOutput, calls=%fused_computation.91 | convolution fusion | flops 812113920 | bytes 11370528 | tf_op jit(solution)/shard_map/cqn,hpn->cqhp/dot_general | solution.py:153
  505.6 3.8 copy.193
  509.4 4.8 reshape.289
  518.8 8.4 %convolution_convert_fusion = bf16[1024,2048]{1,0:T(8,128)(2,1)} fusion(bf16[2,512,2048]{2,1,0:T(8,128)(2,1)} %param.31, f32[1024,512]{1,0:T(8,128)} %copy.181, f32[1024,512]{1,0:T(8,128)} %reshape.289, f32[1024,512]{1,0:T(8,128)} %divide_multiply_fusion, f32[512]{0:T(512)S(1)} %bitcast.266, f32[512]{0:T(512)S(1)} %mul.570, bf16[1024,1024]{1,0:T(8,128)(2,1)} %copy-done.15), kind=kOutput, calls=%fused_computation.65 | convolution fusion | flops 2155347968 | bytes 13635584 | tf_op jit(solution)/shard_map/dot_general | solution.py:166
  527.3 45.6 %reduce-scatter.5.cloned.1.call-done = bf16[1024,512]{1,0:T(8,128)(2,1)} async-done(((bf16[1024,2048]{1,0:T(8,128)(2,1)}), bf16[1024,512]{1,0:T(8,128)(2,1)}) %reduce-scatter.5.cloned.1.call-update) | async-done | bytes 1048592 | tf_op jit(solution)/shard_map/reduce_scatter | solution.py:174
  (286 shorter events, 137.1 us)
Async XLA Ops:
  6.5 193.1 %all-gather.5.cloned.1.call-start = ((), (), s32[]{:S(2)}) async-start(), calls=%async_computation.10 | async-start | bytes 4325376 | tf_op jit(solution)/shard_map/all_gather | solution.py:95
  6.5 26.0 %collective-permute-start = (bf16[1024,512]{1,0:T(8,128)(2,1)}, bf16[1024,512]{1,0:T(8,128)(2,1)S(1)}, u32[]{:S(2)}, u32[]{:S(2)}) collective-permute-start(bf16[1024,512]{1,0:T(8,128)(2,1)} %param.19), channel_id=1, source_target_pairs={{0,1},{1,2},{2,3},{3,0},{4,5},{5,6},{6,7},{7,4},{8,9},{9,10},{10,1... | collective-permute-start | bytes 3145736 | tf_op jit(solution)/shard_map/ppermute | solution.py:21
  8.6 26.0 %collective-permute-start.2 = (bf16[1024,512]{1,0:T(8,128)(2,1)}, bf16[1024,512]{1,0:T(8,128)(2,1)S(1)}, u32[]{:S(2)}, u32[]{:S(2)}) collective-permute-start(bf16[1024,512]{1,0:T(8,128)(2,1)} %param.19), channel_id=1, source_target_pairs={{0,3},{1,0},{2,1},{3,2},{4,7},{5,4},{6,5},{7,6},{8,11},{9,8},{10,9... | collective-permute-start | bytes 3145736 | tf_op jit(solution)/shard_map/ppermute | solution.py:23
  17.8 3.3 copy-start.40
  17.8 15.0 %copy-start.41 = (f32[2,8]{1,0:T(2,128)S(1)}, f32[2,8]{1,0:T(2,128)}, u32[]{:S(2)}) copy-start(f32[2,8]{1,0:T(2,128)} %param.28) | copy-start | bytes 196
  17.8 15.6 %copy-start.25 = (f32[2,4,256]{2,1,0:T(4,128)S(1)}, f32[2,4,256]{2,1,0:T(4,128)}, u32[]{:S(2)}) copy-start(f32[2,4,256]{2,1,0:T(4,128)} %param.26) | copy-start | bytes 24580
  17.8 16.2 %copy-start.21 = (f32[2,4,512]{2,1,0:T(4,128)S(1)}, f32[2,4,512]{2,1,0:T(4,128)}, u32[]{:S(2)}) copy-start(f32[2,4,512]{2,1,0:T(4,128)} %param.25) | copy-start | bytes 49156
  17.8 16.2 %copy-start.22 = (f32[2,2048]{1,0:T(2,128)S(1)}, f32[2,2048]{1,0:T(2,128)}, u32[]{:S(2)}) copy-start(f32[2,2048]{1,0:T(2,128)} %param.21) | copy-start | bytes 49156
  17.8 38.9 %copy-start.12 = (bf16[1024,512]{1,0:T(8,128)(2,1)S(1)}, bf16[1024,512]{1,0:T(8,128)(2,1)}, u32[]{:S(2)}) copy-start(bf16[1024,512]{1,0:T(8,128)(2,1)} %param.19) | copy-start | bytes 3145732
  32.5 24.2 %collective-permute-start.1 = (bf16[1024,512]{1,0:T(8,128)(2,1)S(1)}, bf16[1024,512]{1,0:T(8,128)(2,1)S(1)}, u32[]{:S(2)}, u32[]{:S(2)}) collective-permute-start(bf16[1024,512]{1,0:T(8,128)(2,1)S(1)} %collective-permute-done), channel_id=1, source_target_pairs={{0,1},{1,2},{2,3},{3,0},{4,5},{5,6},{6,7},{7,4},{8,9},{9,10},{10,1... | collective-permute-start | bytes 3145736 | tf_op jit(solution)/shard_map/ppermute | solution.py:21
  34.6 33.6 %copy-start.9 = (bf16[256,8,2,512]{3,1,2,0:T(8,128)(2,1)S(1)}, bf16[256,8,2,512]{3,1,2,0:T(8,128)(2,1)}, u32[]{:S(2)}) copy-start(bf16[256,8,2,512]{3,1,2,0:T(8,128)(2,1)} %copy.200) | copy-start | bytes 12582916
  68.2 7.2 %copy-start.11 = (bf16[1024,2048]{1,0:T(8,128)(2,1)}, bf16[1024,2048]{1,0:T(8,128)(2,1)S(1)}, u32[]{:S(2)}) copy-start(bf16[1024,2048]{1,0:T(8,128)(2,1)S(1)} %get-tuple-element.133) | copy-start | bytes 12582916
  104.7 6.6 %copy-start.20 = (bf16[1024,256]{1,0:T(8,128)(2,1)}, bf16[1024,256]{1,0:T(8,128)(2,1)S(1)}, u32[]{:S(2)}) copy-start(bf16[1024,256]{1,0:T(8,128)(2,1)S(1)} %convolution_convert_fusion.5) | copy-start | bytes 1572868
  105.3 8.4 %collective-permute-start.4 = (bf16[3,256]{1,0:T(4,128)(2,1)}, bf16[3,256]{1,0:T(4,128)(2,1)}, u32[]{:S(2)}, u32[]{:S(2)}) collective-permute-start(bf16[3,256]{1,0:T(4,128)(2,1)} %slice.320), channel_id=1, source_target_pairs={{0,4},{4,8},{8,12},{12,16},{16,20},{20,24},{24,28},{28,32},{32,36}... | collective-permute-start | bytes 4616 | tf_op jit(solution)/shard_map/ppermute | solution.py:46
  111.4 5.8 %collective-permute-start.3 = (bf16[3,512]{1,0:T(4,128)(2,1)}, bf16[3,512]{1,0:T(4,128)(2,1)S(1)}, u32[]{:S(2)}, u32[]{:S(2)}) collective-permute-start(bf16[3,512]{1,0:T(4,128)(2,1)} %slice.314), channel_id=1, source_target_pairs={{0,4},{4,8},{8,12},{12,16},{16,20},{20,24},{24,28},{28,32},{32,36}... | collective-permute-start | bytes 9224 | tf_op jit(solution)/shard_map/ppermute | solution.py:46
  132.7 20.5 %copy-start.42 = (f32[2,8]{1,0:T(2,128)S(1)}, f32[2,8]{1,0:T(2,128)}, u32[]{:S(2)}) copy-start(f32[2,8]{1,0:T(2,128)} %param.29) | copy-start | bytes 196
  132.7 22.3 %copy-start.32 = (f32[2,512]{1,0:T(2,128)S(1)}, f32[2,512]{1,0:T(2,128)}, u32[]{:S(2)}) copy-start(f32[2,512]{1,0:T(2,128)} %param.30) | copy-start | bytes 12292
  156.3 18.7 %all-to-all-start = ((f32[32,1,8]{2,1,0:T(1,128)}), f32[32,1,8]{2,1,0:T(1,128)S(1)}, u32[]{:S(2)}, u32[]{:S(2)}) async-start(f32[32,1,8]{2,1,0:T(1,128)} %broadcast_in_dim.64), calls=%async_computation | async-start | bytes 32768 | tf_op jit(solution)/shard_map/all_to_all | solution.py:36
  164.6 110.3 %reduce-scatter.3.cloned.1.call-start = ((), (), s32[]{:S(2)}) async-start(), calls=%async_computation.8 | async-start | bytes 5242880 | tf_op jit(solution)/shard_map/reduce_scatter | solution.py:174
  170.9 4.2 copy-start.23
  170.9 4.5 copy-start.6
  170.9 5.7 copy-start.4
  176.6 3.2 copy-start.16
  199.6 6.3 %copy-start.1 = (f32[64,8,8,128]{3,2,1,0:T(8,128)S(1)}, f32[64,8,8,128]{3,2,1,0:T(8,128)}, u32[]{:S(2)}) copy-start(f32[64,8,8,128]{3,2,1,0:T(8,128)} %copy-done) | copy-start | bytes 6291460
  199.6 6.3 %copy-start.19 = (f32[8,128,8,64]{1,3,2,0:T(8,128)S(1)}, f32[8,128,8,64]{1,3,2,0:T(8,128)}, u32[]{:S(2)}) copy-start(f32[8,128,8,64]{1,3,2,0:T(8,128)} %copy.159) | copy-start | bytes 6291460
  199.6 6.3 %copy-start.37 = (f32[8]{0:T(128)S(1)}, f32[8]{0:T(128)}, u32[]{:S(2)}) copy-start(f32[8]{0:T(128)} %copy-done.36) | copy-start | bytes 100
  234.4 40.6 %copy-start.13 = (bf16[1024,512]{1,0:T(8,128)(2,1)S(1)}, bf16[1024,512]{1,0:T(8,128)(2,1)}, u32[]{:S(2)}) copy-start(bf16[1024,512]{1,0:T(8,128)(2,1)} %param.19) | copy-start | bytes 3145732
  286.4 23.0 %all-to-all-start.4 = ((bf16[16,2,1,32,512]{4,3,1,2,0:T(8,128)(2,1)}), bf16[16,2,1,32,512]{4,3,1,2,0:T(8,128)(2,1)S(1)}, u32[]{:S(2)}, u32[]{:S(2)}) async-start(bf16[16,2,1,32,512]{4,3,1,2,0:T(8,128)(2,1)} %copy.164), calls=%async_computation.5 | async-start | bytes 2097152 | tf_op jit(solution)/shard_map/all_to_all | solution.py:59
  293.1 200.1 %all-gather.7.cloned.1.call-start = ((), (), s32[]{:S(2)}) async-start(), calls=%async_computation.11 | async-start | bytes 4325376 | tf_op jit(solution)/shard_map/all_gather | solution.py:95
  313.4 23.8 %collective-permute-start.5 = (bf16[1024,512]{1,0:T(8,128)(2,1)S(1)}, bf16[1024,512]{1,0:T(8,128)(2,1)S(1)}, u32[]{:S(2)}, u32[]{:S(2)}) collective-permute-start(bf16[1024,512]{1,0:T(8,128)(2,1)S(1)} %gather_fusion.2), channel_id=1, source_target_pairs={{0,1},{1,2},{2,3},{3,0},{4,5},{5,6},{6,7},{7,4},{8,9},{9,10},{10,1... | collective-permute-start | bytes 3145736 | tf_op jit(solution)/shard_map/ppermute | solution.py:21
  313.5 29.3 %collective-permute-start.7 = (bf16[1024,512]{1,0:T(8,128)(2,1)S(1)}, bf16[1024,512]{1,0:T(8,128)(2,1)}, u32[]{:S(2)}, u32[]{:S(2)}) collective-permute-start(bf16[1024,512]{1,0:T(8,128)(2,1)S(1)} %gather_fusion.2), channel_id=1, source_target_pairs={{0,3},{1,0},{2,1},{3,2},{4,7},{5,4},{6,5},{7,6},{8,11},{9,8},{10,9... | collective-permute-start | bytes 3145736 | tf_op jit(solution)/shard_map/ppermute | solution.py:23
  337.2 23.1 %collective-permute-start.6 = (bf16[1024,512]{1,0:T(8,128)(2,1)S(1)}, bf16[1024,512]{1,0:T(8,128)(2,1)}, u32[]{:S(2)}, u32[]{:S(2)}) collective-permute-start(bf16[1024,512]{1,0:T(8,128)(2,1)S(1)} %collective-permute-done.5), channel_id=1, source_target_pairs={{0,1},{1,2},{2,3},{3,0},{4,5},{5,6},{6,7},{7,4},{8,9},{9,10},{10,1... | collective-permute-start | bytes 3145736 | tf_op jit(solution)/shard_map/ppermute | solution.py:21
  342.8 27.9 %copy-start.26 = (f32[1,2048]{1,0:T(1,128)S(1)}, f32[1,2048]{1,0:T(1,128)}, u32[]{:S(2)}) copy-start(f32[1,2048]{1,0:T(1,128)} %get-tuple-element.160) | copy-start | bytes 24580
  342.8 27.9 %copy-start.44 = (bf16[2,2048,256]{2,1,0:T(8,128)(2,1)S(1)}, bf16[2,2048,256]{2,1,0:T(8,128)(2,1)}, u32[]{:S(2)}) copy-start(bf16[2,2048,256]{2,1,0:T(8,128)(2,1)} %param.23) | copy-start | bytes 6291460
  370.7 7.8 %copy-start.10 = (bf16[1024,2048]{1,0:T(8,128)(2,1)}, bf16[1024,2048]{1,0:T(8,128)(2,1)S(1)}, u32[]{:S(2)}) copy-start(bf16[1024,2048]{1,0:T(8,128)(2,1)S(1)} %get-tuple-element.129) | copy-start | bytes 12582916
  370.7 7.8 %copy-start.43 = (f32[8]{0:T(128)S(1)}, f32[8]{0:T(128)}, u32[]{:S(2)}) copy-start(f32[8]{0:T(128)} %get-tuple-element.179) | copy-start | bytes 100
  370.7 7.8 %copy-start.46 = (bf16[2,2048,8]{1,2,0:T(8,128)(2,1)S(1)}, bf16[2,2048,8]{1,2,0:T(8,128)(2,1)}, u32[]{:S(2)}) copy-start(bf16[2,2048,8]{1,2,0:T(8,128)(2,1)} %param.24) | copy-start | bytes 196612
  372.1 44.2 %collective-permute-start.9 = (bf16[3,256]{1,0:T(4,128)(2,1)S(1)}, bf16[3,256]{1,0:T(4,128)(2,1)S(1)}, u32[]{:S(2)}, u32[]{:S(2)}) collective-permute-start(bf16[3,256]{1,0:T(4,128)(2,1)S(1)} %slice.336), channel_id=1, source_target_pairs={{0,4},{4,8},{8,12},{12,16},{16,20},{20,24},{24,28},{28,32},{32,36}... | collective-permute-start | bytes 4616 | tf_op jit(solution)/shard_map/ppermute | solution.py:46
  413.7 2.7 copy-start.30
  414.1 3.1 collective-permute-start.8
  433.2 15.0 %copy-start.35 = (f32[8]{0:T(128)S(1)}, f32[8]{0:T(128)}, u32[]{:S(2)}) copy-start(f32[8]{0:T(128)} %get-tuple-element.174) | copy-start | bytes 100
  449.0 19.3 %all-to-all-start.5 = ((f32[32,1,8]{2,1,0:T(1,128)}), f32[32,1,8]{2,1,0:T(1,128)S(1)}, u32[]{:S(2)}, u32[]{:S(2)}) async-start(f32[32,1,8]{2,1,0:T(1,128)} %broadcast_in_dim.112), calls=%async_computation.6 | async-start | bytes 32768 | tf_op jit(solution)/shard_map/all_to_all | solution.py:36
  455.8 117.0 %reduce-scatter.5.cloned.1.call-start = ((), (), s32[]{:S(2)}) async-start(), calls=%async_computation.9 | async-start | bytes 5242880 | tf_op jit(solution)/shard_map/reduce_scatter | solution.py:174
  464.1 4.3 copy-start.24
  469.9 4.9 copy-start.17
  493.1 6.0 %copy-start.3 = (f32[64,8,8,128]{3,2,1,0:T(8,128)S(1)}, f32[64,8,8,128]{3,2,1,0:T(8,128)}, u32[]{:S(2)}) copy-start(f32[64,8,8,128]{3,2,1,0:T(8,128)} %copy-done.2) | copy-start | bytes 6291460
  493.2 6.0 %copy-start.18 = (f32[8,128,8,64]{1,3,2,0:T(8,128)S(1)}, f32[8,128,8,64]{1,3,2,0:T(8,128)}, u32[]{:S(2)}) copy-start(f32[8,128,8,64]{1,3,2,0:T(8,128)} %copy.180) | copy-start | bytes 6291460
  515.8 3.0 copy-start.38
  (16 other events, 31.1 us)
Sparse Core Ops, SparseCore 0:
  153.2 46.3 all-gather.4
  229.4 45.4 reduce-scatter.2
  448.3 44.7 all-gather.6
  527.4 45.4 reduce-scatter.4
